TPU v7x, 32 devices: a whole 2x2x4 slice. The times are simulated.
32 devices in a mesh: tile: 8 (over z, x), ka: 4 (over y, core).
Axes of the slice: x: 2, y: 2, z: 4, core: 2. Of those that a mesh axis runs over, the one named last changes fastest.
Arguments:
- amplitudes: bfloat16 [128, 32, 512], P(('tile', 'ka')), may hold values from -6 to 6
- integrals: bfloat16 [64, 512, 4096], P('tile', None, 'ka'), may hold values from -0.046875 to 0.046875
- slot_block: int32 [64], replicated, may hold values from 0 to 32, as said below
- rest: bfloat16 [128, 4096], P('tile', 'ka'), may hold values from -12 to 12
- occ_energy: float32 [128], P('tile'), may hold values from -2 to -0.5
- vir_energy: float32 [4096], P('ka'), may hold values from 0.5 to 3
Outputs:
- new_amp: bfloat16 [128, 4096], P('tile', 'ka')
Inputs may be any that keep to these rules, and one draw needn't show every extreme that they name: `slot_block`: each of the 32 blocks is stored in exactly one slot; the value 32 marks an empty slot. Slots s*8 to s*8 + 7 belong to owner s along tile; an owner holds 0 to 8 blocks, and some owner holds exactly 8.
All inputs are finite; a program needn't handle non-finite values.
Results may differ from a plain program's by a relative error of at most 0.001.
Values may be sent and summed in bfloat16 or wider, within the bound.
A program may use at most 128 MiB of HBM per device.

v0:
```python
import jax
import jax.numpy as jnp
from jax import lax
from jax.sharding import PartitionSpec as P


def per_device(amplitudes, integrals, slot_block, rest, occ_energy, vir_energy):
    capacity = integrals.shape[0]
    block_width = integrals.shape[1]
    tile_count = slot_block.shape[0] // capacity
    nblocks = amplitudes.shape[1]
    picker = (slot_block[:, None] == jnp.arange(nblocks, dtype=jnp.int32)[None, :]).astype(
        jnp.bfloat16
    )
    outgoing = jnp.einsum(
        "sg,rgb->srb", picker, amplitudes, preferred_element_type=jnp.float32
    ).astype(jnp.bfloat16)
    outgoing = outgoing.reshape(tile_count, capacity, amplitudes.shape[0], block_width)
    routed = lax.all_to_all(outgoing, "tile", split_axis=0, concat_axis=0, tiled=True)
    routed = routed[:, None]
    partial_value = jnp.einsum(
        "tksib,sbn->tkin",
        lax.all_gather(routed, "ka", axis=1, tiled=True),
        integrals,
        preferred_element_type=jnp.float32,
    )
    partial_value = partial_value.reshape(-1, partial_value.shape[-1])
    ladder = lax.psum_scatter(partial_value, "tile", scatter_dimension=0, tiled=True)
    denominator = vir_energy[None, :] - occ_energy[:, None]
    return ((rest.astype(jnp.float32) + ladder) / denominator).astype(jnp.bfloat16)


def solution(mesh):
    in_specs = (
        P(("tile", "ka"), None, None),
        P("tile", None, "ka"),
        P(),
        P("tile", "ka"),
        P("tile"),
        P("ka"),
    )
    out_specs = P("tile", "ka")
    return jax.shard_map(
        per_device, mesh=mesh, in_specs=in_specs, out_specs=out_specs, check_vma=False
    )
```

profile of v0, /device:TPU:0, one launch (start us, length us, event | category | flops | bytes accessed | tf_op | source)
XLA Modules:
  0.0 120.0 jit_solution(10600925300919967446)
XLA Ops:
  6.5 0.0 copy-start
  6.5 0.0 copy-start.2
  6.5 0.0 copy-start.3
  6.5 0.0 copy-start.1
  6.5 0.0 all-gather.3.cloned.1.call-start
  6.6 0.9 copy-done
  7.4 0.9 fusion.5
  8.4 16.1 %all_to_all.5 = bf16[8,8,4,512]{3,1,2,0:T(8,128)(2,1)} all-to-all(bf16[8,8,4,512]{3,1,2,0:T(8,128)(2,1)S(1)} %copy.7), channel_id=1, replica_groups=mesh['tile'=8,'ka'=4] {'tile'}, dimensions={0} | all-to-all | bytes 524288 | tf_op jit(solution)/shard_map/all_to_all | solution.py:19
  24.5 0.0 all-gather.3.cloned.1.call-update
  24.5 0.0 reduce-scatter.2.cloned.1.call-start
  24.6 15.8 %all-gather.3.cloned.1.call-done = bf16[8,32,4,512]{3,1,2,0:T(8,128)(2,1)} async-done(((bf16[8,8,4,512]{3,1,2,0:T(8,128)(2,1)}), bf16[8,32,4,512]{3,1,2,0:T(8,128)(2,1)}) %all-gather.3.cloned.1.call-update) | async-done | bytes 1048592 | tf_op jit(solution)/shard_map/all_gather | solution.py:23
  40.4 7.4 %fusion.2 = f32[8,4,4,1024]{3,2,1,0:T(4,128)S(1)} fusion(bf16[8,512,1024]{2,1,0:T(8,128)(2,1)} %param.7, bf16[8,4,8,4,512]{4,2,1,3,0:T(8,128)(2,1)} %bitcast.16), kind=kOutput, calls=%fused_computation.2 | convolution fusion | flops 1073741824 | bytes 9961472 | tf_op jit(solution)/shard_map/tksib,sbn->tkin/dot_general | solution.py:21
  47.9 1.0 reshape.10
  48.8 0.0 reduce-scatter.2.cloned.1.call-update
  48.9 62.8 %reduce-scatter.2.cloned.1.call-done = f32[16,1024]{1,0:T(8,128)} async-done(((f32[128,1024]{1,0:T(8,128)}), f32[16,1024]{1,0:T(8,128)}) %reduce-scatter.2.cloned.1.call-update) | async-done | bytes 65552 | tf_op jit(solution)/shard_map/reduce_scatter | solution.py:28
  111.6 0.0 copy-done.2
  111.6 0.0 copy-done.3
  111.6 0.0 copy-done.1
  111.6 1.5 %divide_convert_fusion = bf16[16,1024]{1,0:T(8,128)(2,1)} fusion(f32[16,1024]{1,0:T(8,128)} %reduce-scatter.2.cloned.1.call-done, bf16[16,1024]{1,0:T(8,128)(2,1)S(1)} %copy-done.1, f32[16]{0:T(128)S(1)} %copy-done.3, f32[1024]{0:T(1024)S(1)} %copy-done.2), kind=kLoop, calls=%fused_computation.6 | loop fusion | flops 81920 | bytes 135232 | tf_op jit(solution)/shard_map/convert_element_type | solution.py:30
  (1 shorter events, 0.0 us)
Async XLA Ops:
  6.5 0.9 copy-start
  6.5 105.1 %copy-start.2 = (f32[1024]{0:T(1024)S(1)}, f32[1024]{0:T(1024)}, u32[]{:S(2)}) copy-start(f32[1024]{0:T(1024)} %param.11) | copy-start | bytes 12292
  6.5 105.1 %copy-start.3 = (f32[16]{0:T(128)S(1)}, f32[16]{0:T(128)}, u32[]{:S(2)}) copy-start(f32[16]{0:T(128)} %param.10) | copy-start | bytes 196
  6.5 105.1 %copy-start.1 = (bf16[16,1024]{1,0:T(8,128)(2,1)S(1)}, bf16[16,1024]{1,0:T(8,128)(2,1)}, u32[]{:S(2)}) copy-start(bf16[16,1024]{1,0:T(8,128)(2,1)} %param.9) | copy-start | bytes 98308
  6.5 33.9 %all-gather.3.cloned.1.call-start = ((), (), s32[]{:S(2)}) async-start(), calls=%async_computation.3 | async-start | bytes 1310720 | tf_op jit(solution)/shard_map/all_gather | solution.py:23
  24.5 87.1 %reduce-scatter.2.cloned.1.call-start = ((), (), s32[]{:S(2)}) async-start(), calls=%async_computation.2 | async-start | bytes 589824 | tf_op jit(solution)/shard_map/reduce_scatter | solution.py:28
Sparse Core Ops, SparseCore 0:
  24.6 15.7 all-gather.2
  49.0 62.6 reduce-scatter.1
where the time goes:
time: 120 us
  waiting for transfers between devices  78.6 us (65%)
  blocking collectives  16.1 us (13%)
  between operations  13.4 us (11%)
  matrix products  8.37 us (7%)
  local copies, waits for them, and re-layouts  1.86 us (2%)
  other arithmetic  1.54 us (1%)
    reduce_scatter x1, waiting for transfers between devices, per_device(): lax.psum_scatter(partial_value, 'tile', scatter_dimension=0, tiled=True)  62.8 us
    all_to_all x1, blocking collectives, per_device(): lax.all_to_all(outgoing, 'tile', split_axis=0, concat_axis=0, tiled=True)  16.1 us
    all_gather x1, waiting for transfers between devices, per_device(): lax.all_gather(routed, 'ka', axis=1, tiled=True)  15.8 us
    dot_general x1, matrix products, per_device(): jnp.einsum('tksib,sbn->tkin', lax.all_gather(routed, 'ka', axis=1, tiled=...  7.44 us
  transfers between devices with their start and end apart: 2, of which 2 were waited for; matrix products, arithmetic and copies ran while one was open for 0% of the time, Pallas kernels for 0%

commit v1 on v0

v1 whole, which is shorter than its diff:
```python
import functools

import jax
import jax.numpy as jnp
from jax import lax
from jax.experimental import pallas as pl
from jax.experimental.pallas import tpu as pltpu
from jax.sharding import PartitionSpec as P

MESH = pl.DeviceIdType.MESH
UNROLL = 8


def repeat(count, body):
    if count <= UNROLL:
        for index in range(count):
            body(index)
    else:
        pl.loop(0, count)(body)


def kernel(tiles, fan, chunks, slots_ref, amp_ref, rest_ref, occ_ref, vir_ref, int_ref, out_ref,
           wide, outgoing, arrived, lhs_peer, lhs_own, blocks, pair_send, pair_recv, line_send, line_recv,
           int_sem, self_sem, direct_sem, recv_sem, fwd_sem, pair_sem, pair_rsem, line_sem, line_rsem):
    me, k = lax.axis_index("tile"), lax.axis_index("ka")
    rows, nblocks, width = amp_ref.shape
    capacity = int_ref.shape[0]
    half = tiles // 2
    group = fan * rows
    span = out_ref.shape[1] // chunks

    fills = [pltpu.make_async_copy(int_ref.at[s], blocks.at[s], int_sem.at[s]) for s in range(capacity)]

    barrier = pltpu.get_barrier_semaphore()

    def greet(m):
        pl.semaphore_signal(barrier, inc=1, device_id={"tile": me ^ m}, device_id_type=MESH)

    repeat(tiles - 1, lambda i: greet(i + 1))
    bits = []
    bit = fan // 2
    while bit:
        bits.append(bit)
        bit //= 2
    for bit in bits:
        pl.semaphore_signal(barrier, inc=1, device_id={"ka": k ^ bit}, device_id_type=MESH)
    for fill in fills:
        fill.start()

    for r in range(rows):
        for lane in range(width // 128):
            part = amp_ref[r, :, pl.ds(lane * 128, 128)].astype(jnp.float32)
            wide[lane, pl.ds(r * nblocks, nblocks), :] = part

    def gather(m):
        for s in range(capacity):
            block = slots_ref[(me ^ m) * capacity + s]
            start = jnp.minimum(block, nblocks - 1)
            for lane in range(width // 128):
                picked = wide[lane, pl.ds(start, rows, stride=nblocks), :]
                picked = jnp.where(block < nblocks, picked, 0.0)
                outgoing[m, :, pl.ds(s * width + lane * 128, 128)] = picked.astype(jnp.bfloat16)

    repeat(tiles, gather)
    pl.semaphore_wait(barrier, tiles - 1 + len(bits))

    def direct(m):
        return pltpu.make_async_remote_copy(
            src_ref=outgoing.at[m], dst_ref=arrived.at[m, k], send_sem=direct_sem.at[m],
            recv_sem=recv_sem.at[m, 0], device_id={"tile": me ^ m}, device_id_type=MESH)

    def forward(m, q, bit, own=False):
        source = outgoing.at[m] if own else arrived.at[m, k ^ q]
        return pltpu.make_async_remote_copy(
            src_ref=source, dst_ref=arrived.at[m, k ^ q], send_sem=fwd_sem.at[m, q | bit],
            recv_sem=recv_sem.at[m, q | bit], device_id={"ka": k ^ bit}, device_id_type=MESH)

    keep = pltpu.make_async_copy(outgoing.at[0], arrived.at[0, k], self_sem)
    keep.start()

    def spread(m, own=False):
        for bit in bits:
            forward(m, 0, bit, own).start()

    def relay(m):
        for high in range(len(bits) - 1):
            top = bits[high]
            for rest_q in range(0, fan, 2 * top):
                q = rest_q | top
                forward_wait(m, q)
                for bit in bits[high + 1:]:
                    forward(m, q, bit).start()

    def forward_wait(m, q):
        pltpu.make_async_remote_copy(
            src_ref=arrived.at[m, k], dst_ref=arrived.at[m, k], send_sem=fwd_sem.at[m, q],
            recv_sem=recv_sem.at[m, q], device_id={"ka": k ^ 1}, device_id_type=MESH).wait_recv()

    spread(0, own=True)
    repeat(half, lambda i: direct(tiles - 1 - 2 * i).start())
    repeat(half - 1, lambda i: direct(tiles - 2 - 2 * i).start())

    def take(m):
        direct(m).wait_recv()
        spread(m)

    def step_peer(i):
        take(tiles - 1 - 2 * i)

    repeat(half, step_peer)
    relay(0)

    def step_own(i):
        relay(tiles - 1 - 2 * i)
        take(tiles - 2 - 2 * i)

    repeat(half - 1, step_own)
    relay(1)
    repeat(half - 1, lambda i: relay(tiles - 2 - 2 * i))

    def finish(m):
        for q in range(1, fan):
            if q & 1:
                forward_wait(m, q)

    def assemble(m, target, j):
        pieces = [arrived[m, q].astype(jnp.float32) for q in range(fan)]
        target[pl.ds(j * group, group), :] = jnp.concatenate(pieces, axis=0).astype(jnp.bfloat16)

    def ready_peer(i):
        m = tiles - 1 - 2 * i
        finish(m)
        assemble(m, lhs_peer, half - 1 - i)

    repeat(half, ready_peer)
    for fill in fills:
        fill.wait()

    total = half * group
    piece = min(total, 128)

    def product(source, c, base):
        acc = None
        for s in range(capacity):
            term = jnp.dot(source[pl.ds(base, piece), pl.ds(s * width, width)],
                           blocks[s, :, pl.ds(c * span, span)], preferred_element_type=jnp.float32)
            acc = term if acc is None else acc + term
        return acc

    def pair(c):
        return pltpu.make_async_remote_copy(
            src_ref=pair_send.at[c], dst_ref=pair_recv.at[c], send_sem=pair_sem.at[c],
            recv_sem=pair_rsem.at[c], device_id={"tile": me ^ 1}, device_id_type=MESH)

    def line(c, j):
        return pltpu.make_async_remote_copy(
            src_ref=line_send.at[c, pl.ds(j * group, group)], dst_ref=line_recv.at[c, j],
            send_sem=line_sem.at[c, j], recv_sem=line_rsem.at[c, j],
            device_id={"tile": me ^ (2 * j)}, device_id_type=MESH)

    for c in range(chunks):
        def fill_pair(b):
            base = b * piece
            pair_send[c, pl.ds(base, piece), :] = product(lhs_peer, c, base)
        repeat(total // piece, fill_pair)
        pair(c).start()

    keep.wait()
    for q in range(1, fan):
        if q & 1:
            forward_wait(0, q)
    assemble(0, lhs_own, 0)

    def ready_own(i):
        m = tiles - 2 - 2 * i
        finish(m)
        assemble(m, lhs_own, half - 1 - i)

    repeat(half - 1, ready_own)

    for c in range(chunks):
        def fill_line(b):
            base = b * piece
            line_send[c, pl.ds(base, piece), :] = product(lhs_own, c, base)
        repeat(total // piece, fill_line)
        pair(c).wait_recv()

        def add_line(b):
            base = b * piece
            line_send[c, pl.ds(base, piece), :] += pair_recv[c, pl.ds(base, piece), :]
        repeat(total // piece, add_line)
        repeat(half - 1, lambda i: line(c, half - 1 - i).start())

    eye = lax.broadcasted_iota(jnp.int32, (group, group), 0) == lax.broadcasted_iota(jnp.int32, (group, group), 1)
    occ = jnp.sum(jnp.where(eye, occ_ref[...], 0.0), axis=1, keepdims=True)
    for c in range(chunks):
        columns = pl.ds(c * span, span)
        ladder = line_send[c, pl.ds(0, group), :]
        for j in range(1, half):
            line(c, j).wait_recv()
            ladder = ladder + line_recv[c, j]
        value = rest_ref[:, columns].astype(jnp.float32) + ladder
        out_ref[:, columns] = (value / (vir_ref[:, columns] - occ)).astype(out_ref.dtype)

    repeat(tiles - 1, lambda i: direct(i + 1).wait_send())

    def drain(m):
        for q in range(1, fan):
            pltpu.make_async_remote_copy(
                src_ref=arrived.at[m, k], dst_ref=arrived.at[m, k], send_sem=fwd_sem.at[m, q],
                recv_sem=recv_sem.at[m, q], device_id={"ka": k ^ 1}, device_id_type=MESH).wait_send()

    repeat(tiles, drain)
    for c in range(chunks):
        pair(c).wait_send()
        repeat(half - 1, lambda i: line(c, i + 1).wait_send())


def per_device(tiles, fan, amplitudes, integrals, slot_block, rest, occ_energy, vir_energy):
    rows, nblocks, width = amplitudes.shape
    capacity, _, columns = integrals.shape
    half, group = tiles // 2, fan * rows
    chunks = 4
    span = columns // chunks
    vmem = pl.BlockSpec(memory_space=pltpu.VMEM)
    f32, bf16 = jnp.float32, jnp.bfloat16
    dma = pltpu.SemaphoreType.DMA
    return pl.pallas_call(
        functools.partial(kernel, tiles, fan, chunks),
        out_shape=jax.ShapeDtypeStruct(rest.shape, bf16),
        in_specs=[pl.BlockSpec(memory_space=pltpu.SMEM), vmem, vmem, vmem, vmem, pl.BlockSpec(memory_space=pl.ANY)],
        out_specs=vmem,
        scratch_shapes=[
            pltpu.VMEM((width // 128, rows * nblocks, 128), f32),
            pltpu.VMEM((tiles, rows, capacity * width), bf16),
            pltpu.VMEM((tiles, fan, rows, capacity * width), bf16),
            pltpu.VMEM((half * group, capacity * width), bf16),
            pltpu.VMEM((half * group, capacity * width), bf16),
            pltpu.VMEM((capacity, width, columns), bf16),
            pltpu.VMEM((chunks, half * group, span), f32),
            pltpu.VMEM((chunks, half * group, span), f32),
            pltpu.VMEM((chunks, half * group, span), f32),
            pltpu.VMEM((chunks, half, group, span), f32),
            dma((capacity,)),
            dma,
            dma((tiles,)),
            dma((tiles, fan)),
            dma((tiles, fan)),
            dma((chunks,)),
            dma((chunks,)),
            dma((chunks, half)),
            dma((chunks, half)),
        ],
        compiler_params=pltpu.CompilerParams(
            collective_id=0, has_side_effects=True, vmem_limit_bytes=60 * 1024 * 1024),
    )(slot_block, amplitudes, rest, occ_energy.reshape(1, -1), vir_energy.reshape(1, -1), integrals)


def solution(mesh):
    in_specs = (
        P(("tile", "ka"), None, None),
        P("tile", None, "ka"),
        P(),
        P("tile", "ka"),
        P("tile"),
        P("ka"),
    )
    body = functools.partial(per_device, mesh.shape["tile"], mesh.shape["ka"])
    return jax.shard_map(body, mesh=mesh, in_specs=in_specs, out_specs=P("tile", "ka"), check_vma=False)
```

time: 120 us -> 34.4 us (0.29)
  waiting for transfers between devices: 78.6 us -> 0 us
  Pallas kernels: 0 us -> 32.8 us
  blocking collectives: 16.1 us -> 0 us
  between operations: 13.4 us -> 0.01 us
  matrix products: 8.37 us -> 0 us
  other arithmetic: 1.54 us -> 0 us
    reduce_scatter x1 -> x0, waiting for transfers between devices: 62.8 us -> none  [per_device(): lax.psum_scatter(partial_value, 'tile', scatter_dimension=0, tiled=True)]
    pallas_call x0 -> x1, Pallas kernels: none -> 32.8 us  [per_device(): pl.pallas_call(functools.partial(kernel, tiles, fan, chunks), out_shape=j...]
    all_to_all x1 -> x0, blocking collectives: 16.1 us -> none  [per_device(): lax.all_to_all(outgoing, 'tile', split_axis=0, concat_axis=0, tiled=True)]
    all_gather x1 -> x0, waiting for transfers between devices: 15.8 us -> none  [per_device(): lax.all_gather(routed, 'ka', axis=1, tiled=True)]
    dot_general x2 -> x0, matrix products: 8.37 us -> none  [the longest x1 7.44 us: per_device(): jnp.einsum('tksib,sbn->tkin', lax.all_gather(routed, 'ka', axis=1, tiled=...]
    convert_element_type x1 -> x0, other arithmetic: 1.54 us -> none  [per_device(): ((rest.astype(jnp.float32) + ladder) / denominator).astype(jnp.bfloat16)]
  transfers between devices with their start and end apart: 2 -> 0, of which waited for: 2 -> 0; matrix products, arithmetic and copies ran while one was open for 0% -> 0% of each run, Pallas kernels for 0% -> 0%
where the time goes in v1:
time: 34.4 us; the launch traced here: 34.2 us
  Pallas kernels  32.8 us (95%)
  local copies, waits for them, and re-layouts  1.38 us (4%)
    pallas_call x1, Pallas kernels, per_device(): pl.pallas_call(functools.partial(kernel, tiles, fan, chunks), out_shape=j...  32.8 us
    unnamed x1, local copies, waits for them, and re-layouts  1.38 us

profile of v1, /device:TPU:0, one launch (start us, length us, event | category | flops | bytes accessed | tf_op | source)
XLA Modules:
  0.0 34.2 jit_solution(1829802489895774275)
XLA Ops:
  0.0 32.8 %shard_map.64 = bf16[16,1024]{1,0:T(8,128)(2,1)} custom-call(s32[64]{0:T(128)} %slots_ref.1, bf16[4,32,512]{2,1,0:T(8,128)(2,1)} %amp_ref.1, bf16[16,1024]{1,0:T(8,128)(2,1)} %rest_ref.1, f32[1,16]{1,0:T(1,128)} %bitcast.3, f32[1,1024]{1,0:T(1,128)} %bitcast.2, bf16[8,512,1024]{2,1,0:T(8,128)(2,1)} %int_ref.1), custom_call_target="tpu_custom_call" | custom-call | tf_op jit(solution)/shard_map/pallas_call | solution.py:228
  32.9 1.4 %copy.8 = bf16[16,1024]{1,0:T(8,128)(2,1)} copy(bf16[16,1024]{1,0:T(8,128)(2,1)} %shard_map.64) | data formatting | bytes 65536
